TPU v7x, 512 devices: a whole 4x8x8 slice. The times are simulated.
512 devices in a mesh: layer: 16 (over z, core), plane: 32 (over x, y).
Axes of the slice: x: 4, y: 8, z: 8, core: 2. Of those that a mesh axis runs over, the one named last changes fastest.
Arguments:
- velocity: bfloat16 [2, 128, 131072], P(None, 'layer', 'plane'), may hold values from -6 to 6
- adjoint: bfloat16 [2, 128, 131072], P(None, 'layer', 'plane'), may hold values from -6 to 6
- corners: int32 [4, 131072], P(None, 'plane'), may hold values from 0 to 4607, as said below
- shared: int32 [4, 4096], P(None, 'plane'), may hold values from 0 to 4096, as said below
- stretch: float32 [2, 131072], P(None, 'plane'), may hold values from 0.5 to 2
- shear_part: float32 [2, 131072], P(None, 'plane'), may hold values from -0.2 to 0.2
- thickness: float32 [128, 131072], P('layer', 'plane'), may hold values from 0.3 to 3
- rate_factor: float32 [128, 131072], P('layer', 'plane'), may hold values from 0.5 to 2
- retention: float32 [128, 131072], P('layer', 'plane'), may hold values from 0.2 to 1
- weight: float32 [128, 131072], P('layer', 'plane'), may hold values from 0.5 to 2
Outputs:
- gradient: float32 [131072], P('plane')
Inputs may be any that keep to these rules, and one draw needn't show every extreme that they name: `corners`: below 4096 a number names an owned node; 4096 + j * 128 + s names slot s of the ghost block of direction j (plane offsets -2, -1, +1, +2). Every slot of a block whose partition exists is named by exactly one corner, corner 0 of some element; blocks of directions beyond the ends of the plane axis are named by none. `shared`: row j, block p lists 128 distinct owned nodes of partition p that the partition at offset o_j (-2, -1, +1, +2) holds as ghosts; the block is 4096 throughout where that partition does not exist.
All inputs are finite; a program needn't handle non-finite values.
Results may differ from a plain program's by a relative error of at most 0.0003.
Values may be sent and summed in bfloat16 or wider, within the bound.
A program may use at most 128 MiB of HBM per device.

v0:
```python
import math
import jax
import jax.numpy as jnp
from jax import lax
from jax.sharding import PartitionSpec as P

OFFSETS = (-2, -1, 1, 2)
STRAIN_EPS = 0.01
LOW_SPAN = 64


def shifted(value, axis, steps):
    count = lax.axis_size(axis)
    first, last = (max(0, -steps), min(count, count - steps))
    return lax.ppermute(value, axis, [(source, source + steps) for source in range(first, last)])


def entering_2(value, axis, combine, identity):
    devices, place = (lax.axis_size(axis), lax.axis_index(axis))
    everything = jax.tree.map(lambda part: lax.all_gather(part, axis), value)
    start = jax.tree.map(
        lambda part, zero: jnp.broadcast_to(jnp.asarray(zero, part.dtype), part.shape),
        value,
        identity,
    )

    def hop(k, before):
        reached = k < place
        new = combine(before, jax.tree.map(lambda part: part[k], everything))
        return jax.tree.map(lambda a, b: jnp.where(reached, a, b), new, before)

    return lax.fori_loop(0, devices, hop, start)


def basis_table():
    gauss_point = 1.0 / math.sqrt(3.0)
    xi_signs = [-1.0, 1.0, 1.0, -1.0, -1.0, 1.0, 1.0, -1.0]
    eta_signs = [-1.0, -1.0, 1.0, 1.0, -1.0, -1.0, 1.0, 1.0]
    zeta_signs = [1.0, 1.0, 1.0, 1.0, -1.0, -1.0, -1.0, -1.0]
    shape_table = [[0.0] * 8 for row_index in range(24)]
    for point_index in range(8):
        xi_point = gauss_point if point_index & 1 else -gauss_point
        eta_point = gauss_point if point_index & 2 else -gauss_point
        zeta_point = gauss_point if point_index & 4 else -gauss_point
        for node_index in range(8):
            along_xi = 1.0 + xi_signs[node_index] * xi_point
            along_eta = 1.0 + eta_signs[node_index] * eta_point
            along_zeta = 1.0 + zeta_signs[node_index] * zeta_point
            shape_table[point_index][node_index] = (
                xi_signs[node_index] * along_eta * along_zeta / 8.0
            )
            shape_table[8 + point_index][node_index] = (
                eta_signs[node_index] * along_xi * along_zeta / 8.0
            )
            shape_table[16 + point_index][node_index] = (
                zeta_signs[node_index] * along_xi * along_eta / 8.0
            )
    return shape_table


def strain_of(grad_x, grad_y, grad_z, first_comp, second_comp):
    return (
        grad_x[first_comp],
        grad_y[second_comp],
        0.5 * (grad_y[first_comp] + grad_x[second_comp]),
        0.5 * grad_z[first_comp],
        0.5 * grad_z[second_comp],
    )


def pairing(left_strain, right_strain):
    return (
        left_strain[0] * right_strain[0]
        + left_strain[1] * right_strain[1]
        + 0.5 * (left_strain[0] * right_strain[1] + left_strain[1] * right_strain[0])
        + left_strain[2] * right_strain[2]
        + left_strain[3] * right_strain[3]
        + left_strain[4] * right_strain[4]
    )


def element_terms(nodal_values, stretch, shear_part, thickness, rate_factor):
    layer_count = nodal_values.shape[1] - 1
    width = nodal_values.shape[3]
    top_nodes = nodal_values[:, :-1]
    bottom_nodes = nodal_values[:, 1:]
    hexa_nodes = jnp.concatenate([top_nodes, bottom_nodes], axis=2)
    basis = jnp.asarray(basis_table(), dtype=jnp.float32)
    derived = jnp.einsum("rn,clnb->clrb", basis, hexa_nodes, precision=lax.Precision.HIGHEST)
    derived = derived.reshape(4, layer_count, 3, 8, width)
    along_xi = derived[:, :, 0]
    along_eta = derived[:, :, 1]
    along_zeta = derived[:, :, 2]
    grad_x = stretch[0] * along_xi + shear_part[0] * along_eta
    grad_y = shear_part[1] * along_xi + stretch[1] * along_eta
    grad_z = (2.0 / thickness)[None, :, None, :] * along_zeta
    flow_strain = strain_of(grad_x, grad_y, grad_z, 0, 1)
    adjoint_strain = strain_of(grad_x, grad_y, grad_z, 2, 3)
    effective = pairing(flow_strain, flow_strain) + STRAIN_EPS
    viscosity = 0.5 * rate_factor[:, None, :] * jnp.power(effective, -1.0 / 3.0)
    volume = 0.5 * thickness / (stretch[0] * stretch[1] - shear_part[0] * shear_part[1])
    return volume * jnp.sum(4.0 * viscosity * pairing(flow_strain, adjoint_strain), axis=1)


def high_select(node_ids, high_count, dtype):
    high_part = node_ids // LOW_SPAN
    return (jnp.arange(high_count, dtype=jnp.int32)[:, None] == high_part[None, :]).astype(dtype)


def low_select(node_ids):
    low_part = node_ids % LOW_SPAN
    return (jnp.arange(LOW_SPAN, dtype=jnp.int32)[:, None] == low_part[None, :]).astype(jnp.float32)


def compose(earlier, later):
    return (earlier[0] * later[0], later[0] * earlier[1] + later[1])


def shards(
    velocity,
    adjoint,
    corners,
    shared,
    stretch,
    shear_part,
    thickness,
    rate_factor,
    retention,
    weight,
):
    owned_count = velocity.shape[2]
    layer_count = velocity.shape[1]
    slot_count = shared.shape[1]
    elem_count = corners.shape[1]
    fields = jnp.concatenate([velocity, adjoint], axis=0)
    padded = jnp.concatenate([fields, jnp.zeros((4, layer_count, 1), fields.dtype)], axis=2)
    outgoing = [jnp.take(padded, shared[direction], axis=2) for direction in range(4)]
    incoming = [
        shifted(outgoing[3 - direction], "plane", -OFFSETS[direction]) for direction in range(4)
    ]
    local_fields = jnp.concatenate([fields] + incoming, axis=2)
    local_count = local_fields.shape[2]
    high_count = local_count // LOW_SPAN
    below_level = shifted(local_fields[:, 0], "layer", -1)
    levels = jnp.concatenate([local_fields, below_level[:, None]], axis=1)
    level_rows = 4 * (layer_count + 1)
    level_table = levels.reshape(level_rows, high_count, LOW_SPAN)
    level_table = jnp.transpose(level_table, (0, 2, 1)).reshape(level_rows * LOW_SPAN, high_count)
    block_size = min(1024, elem_count)
    block_count = elem_count // block_size

    def one_block(block_start):
        corner_ids = lax.dynamic_slice_in_dim(corners, block_start, block_size, 1).reshape(-1)
        picked = jnp.dot(
            level_table,
            high_select(corner_ids, high_count, jnp.bfloat16),
            preferred_element_type=jnp.float32,
        )
        picked = picked.reshape(level_rows, LOW_SPAN, 4 * block_size)
        nodal_values = jnp.sum(picked * low_select(corner_ids)[None], axis=1)
        nodal_values = nodal_values.reshape(4, layer_count + 1, 4, block_size)
        return element_terms(
            nodal_values,
            lax.dynamic_slice_in_dim(stretch, block_start, block_size, 1),
            lax.dynamic_slice_in_dim(shear_part, block_start, block_size, 1),
            lax.dynamic_slice_in_dim(thickness, block_start, block_size, 1),
            lax.dynamic_slice_in_dim(rate_factor, block_start, block_size, 1),
        )

    layer_terms = lax.map(one_block, jnp.arange(block_count, dtype=jnp.int32) * block_size)
    layer_terms = jnp.transpose(layer_terms, (1, 0, 2)).reshape(layer_count, elem_count)
    factor = jnp.ones((elem_count,), jnp.float32)
    offset = jnp.zeros((elem_count,), jnp.float32)
    for layer_index in range(layer_count):
        factor = retention[layer_index] * factor
        offset = (
            retention[layer_index] * offset + (1.0 - retention[layer_index]) * weight[layer_index]
        )
    identity = (jnp.ones((elem_count,), jnp.float32), jnp.zeros((elem_count,), jnp.float32))
    _, entering = entering_2((factor, offset), "layer", compose, identity)
    running = entering
    column = jnp.zeros((elem_count,), jnp.float32)
    for layer_index in range(layer_count):
        running = (
            retention[layer_index] * running + (1.0 - retention[layer_index]) * weight[layer_index]
        )
        column = column + running * layer_terms[layer_index]
    quarter = 0.25 * column

    def add_block(block_index, node_table):
        block_start = block_index * block_size
        corner_ids = lax.dynamic_slice_in_dim(corners, block_start, block_size, 1).reshape(-1)
        values = jnp.tile(lax.dynamic_slice_in_dim(quarter, block_start, block_size, 0), 4)
        low_values = low_select(corner_ids) * values[None, :]
        return node_table + jnp.dot(
            low_values,
            high_select(corner_ids, high_count, jnp.float32).T,
            precision=lax.Precision.HIGHEST,
            preferred_element_type=jnp.float32,
        )

    node_table = lax.fori_loop(
        0, block_count, add_block, jnp.zeros((LOW_SPAN, high_count), jnp.float32)
    )
    partial_nodes = jnp.transpose(node_table).reshape(local_count)
    summed = lax.psum(partial_nodes, "layer")
    ghost_part = summed[owned_count:].reshape(4, slot_count)
    arriving = [
        shifted(ghost_part[3 - direction], "plane", -OFFSETS[direction]) for direction in range(4)
    ]
    owned_sum = jnp.concatenate([summed[:owned_count], jnp.zeros((1,), jnp.float32)])
    for direction in range(4):
        owned_sum = owned_sum.at[shared[direction]].add(arriving[direction])
    return owned_sum[:owned_count]


def solution(mesh):
    return jax.shard_map(
        shards,
        mesh=mesh,
        in_specs=(
            P(None, "layer", "plane"),
            P(None, "layer", "plane"),
            P(None, "plane"),
            P(None, "plane"),
            P(None, "plane"),
            P(None, "plane"),
            P("layer", "plane"),
            P("layer", "plane"),
            P("layer", "plane"),
            P("layer", "plane"),
        ),
        out_specs=P("plane"),
        check_vma=False,
    )
```

profile of v0, /device:TPU:2, one launch (start us, length us, event | category | flops | bytes accessed | tf_op | source)
XLA Modules:
  0.0 332.4 jit_solution(698319157925830426)
XLA Ops:
  1.9 4.6 %copy.48 = bf16[4,8,4096]{1,0,2:T(4,128)(2,1)} copy(bf16[4,8,4096]{2,1,0:T(8,128)(2,1)S(1)} %pad_maximum_fusion.1) | data formatting | bytes 524288 | tf_op jit(solution)/shard_map/concatenate | solution.py:135
  6.5 6.8 %concatenate.22 = bf16[4,8,4097]{1,0,2:T(4,128)(2,1)} pad(bf16[4,8,4096]{1,0,2:T(4,128)(2,1)} %copy.48, bf16[]{:T(256)} %constant.242.clone.1), padding=0_0x0_0x0_1 | pad | bytes 524354 | tf_op jit(solution)/shard_map/concatenate | solution.py:136
  13.3 3.0 gather_fusion
  16.5 4.5 %collective-permute-start = (bf16[4,8,128]{1,0,2:T(4,128)(2,1)S(1)}, bf16[4,8,128]{1,0,2:T(4,128)(2,1)S(1)}, u32[]{:S(2)}, u32[]{:S(2)}) collective-permute-start(bf16[4,8,128]{1,0,2:T(4,128)(2,1)S(1)} %select_bitcast_fusion.3), channel_id=1, source_target_pairs={{0,2},{1,3},{2,4},{3,5},{4,6},{5,7},{6,8},{7,9},{8,10},{9,11},{10,... | collective-permute-start | bytes 24584 | tf_op jit(solution)/shard_map/ppermute | solution.py:15
  21.0 2.9 gather_fusion.1
  24.2 3.5 %collective-permute-start.1 = (bf16[4,8,128]{1,0,2:T(4,128)(2,1)S(1)}, bf16[4,8,128]{1,0,2:T(4,128)(2,1)S(1)}, u32[]{:S(2)}, u32[]{:S(2)}) collective-permute-start(bf16[4,8,128]{1,0,2:T(4,128)(2,1)S(1)} %select_bitcast_fusion.2), channel_id=1, source_target_pairs={{0,1},{1,2},{2,3},{3,4},{4,5},{5,6},{6,7},{7,8},{8,9},{9,10},{10,1... | collective-permute-start | bytes 24584 | tf_op jit(solution)/shard_map/ppermute | solution.py:15
  27.7 2.9 gather_fusion.2
  30.8 4.5 %collective-permute-start.2 = (bf16[4,8,128]{1,0,2:T(4,128)(2,1)S(1)}, bf16[4,8,128]{1,0,2:T(4,128)(2,1)S(1)}, u32[]{:S(2)}, u32[]{:S(2)}) collective-permute-start(bf16[4,8,128]{1,0,2:T(4,128)(2,1)S(1)} %select_bitcast_fusion.1), channel_id=1, source_target_pairs={{1,0},{2,1},{3,2},{4,3},{5,4},{6,5},{7,6},{8,7},{9,8},{10,9},{11,1... | collective-permute-start | bytes 24584 | tf_op jit(solution)/shard_map/ppermute | solution.py:15
  35.3 2.9 gather_fusion.3
  38.5 2.4 collective-permute-start.3
  43.3 23.9 %all-gather = f32[16,1,4096]{2,1,0:T(1,128)S(1)} all-gather(f32[1,1,4096]{2,1,0:T(1,128)S(1)} %get-tuple-element.500), channel_id=1, replica_groups=mesh['layer'=16,'plane'=32] {'layer'}, dimensions={0}, use_global_device_ids=true | all-gather | bytes 278528 | tf_op jit(solution)/shard_map/all_gather | solution.py:20
  67.3 15.2 %all-gather.1 = f32[16,1,4096]{2,1,0:T(1,128)S(1)} all-gather(f32[1,1,4096]{2,1,0:T(1,128)S(1)} %get-tuple-element.496), channel_id=1, replica_groups=mesh['layer'=16,'plane'=32] {'layer'}, dimensions={0}, use_global_device_ids=true | all-gather | bytes 278528 | tf_op jit(solution)/shard_map/all_gather | solution.py:20
  89.8 163.1 %while.43 = (s32[]{:T(128)}, f32[4,8,1024]{2,1,0:T(8,128)S(1)}, s32[4]{0:T(128)S(1)}, f32[8,4096]{1,0:T(8,128)S(1)}, f32[2,4096]{1,0:T(2,128)}, /*index=5*/f32[2...) while((s32[]{:T(128)}, f32[4,8,1024]{2,1,0:T(8,128)S(1)}, ...), condition=%wide.region_5.7_spmd.clone, body=%wide.region_2.6_spmd.sunk.clone.sunk | while | flops 1458830336 | bytes 95925216 | solution.py:170
  92.4 16.0 %fusion.57 = f32[4096,2304]{0,1:T(8,128)} fusion(bf16[2304,72]{1,0:T(8,128)(2,1)} %get-tuple-element.719, s32[4096]{0:T(1024)S(1)} %get-tuple-element.656), kind=kOutput, calls=%fused_computation.11.clone.1 | convolution fusion | flops 1359249408 | bytes 38096896 | tf_op jit(solution)/shard_map/while/body/eval_jaxpr/dot_general | solution.py:154
  108.5 14.8 %multiply_reduce_fusion.2 = f32[36,4096]{1,0:T(8,128)S(1)} fusion(f32[36,64,4096]{2,1,0:T(8,128)} %bitcast.239, f32[64,4096]{1,0:T(8,128)S(1)} %fusion.58), kind=kLoop, calls=%fused_computation.8.clone.1 | loop fusion | flops 18726912 | bytes 39387136 | tf_op jit(solution)/shard_map/while/body/eval_jaxpr/reduce_sum | solution.py:160
  124.0 3.6 %convolution_bitcast_fusion.2 = f32[4,8,3,8,1024]{4,3,2,1,0:T(8,128)S(1)} fusion(f32[24,8,1,1]{0,1,3,2:T(8,128)S(1)} %get-tuple-element.721, f32[4,8,4,1024]{3,2,1,0:T(4,128)S(1)} %get-tuple-element.658, f32[4,8,4,1024]{3,2,1,0:T(4,128)S(1)} %get-tuple-element.659), kind=kOutput, calls=%fused_computation.9.clone.1 | convolution fusion | flops 75759616 | bytes 4195072 | tf_op jit(solution)/shard_map/while/body/eval_jaxpr/rn,clnb->clrb/dot_general | solution.py:89
  133.2 16.0 %fusion.57 = f32[4096,2304]{0,1:T(8,128)} fusion(bf16[2304,72]{1,0:T(8,128)(2,1)} %get-tuple-element.719, s32[4096]{0:T(1024)S(1)} %get-tuple-element.656), kind=kOutput, calls=%fused_computation.11.clone.1 | convolution fusion | flops 1359249408 | bytes 38096896 | tf_op jit(solution)/shard_map/while/body/eval_jaxpr/dot_general | solution.py:154
  149.3 14.8 %multiply_reduce_fusion.2 = f32[36,4096]{1,0:T(8,128)S(1)} fusion(f32[36,64,4096]{2,1,0:T(8,128)} %bitcast.239, f32[64,4096]{1,0:T(8,128)S(1)} %fusion.58), kind=kLoop, calls=%fused_computation.8.clone.1 | loop fusion | flops 18726912 | bytes 39387136 | tf_op jit(solution)/shard_map/while/body/eval_jaxpr/reduce_sum | solution.py:160
  164.7 3.6 %convolution_bitcast_fusion.2 = f32[4,8,3,8,1024]{4,3,2,1,0:T(8,128)S(1)} fusion(f32[24,8,1,1]{0,1,3,2:T(8,128)S(1)} %get-tuple-element.721, f32[4,8,4,1024]{3,2,1,0:T(4,128)S(1)} %get-tuple-element.658, f32[4,8,4,1024]{3,2,1,0:T(4,128)S(1)} %get-tuple-element.659), kind=kOutput, calls=%fused_computation.9.clone.1 | convolution fusion | flops 75759616 | bytes 4195072 | tf_op jit(solution)/shard_map/while/body/eval_jaxpr/rn,clnb->clrb/dot_general | solution.py:89
  174.0 16.0 %fusion.57 = f32[4096,2304]{0,1:T(8,128)} fusion(bf16[2304,72]{1,0:T(8,128)(2,1)} %get-tuple-element.719, s32[4096]{0:T(1024)S(1)} %get-tuple-element.656), kind=kOutput, calls=%fused_computation.11.clone.1 | convolution fusion | flops 1359249408 | bytes 38096896 | tf_op jit(solution)/shard_map/while/body/eval_jaxpr/dot_general | solution.py:154
  190.1 14.8 %multiply_reduce_fusion.2 = f32[36,4096]{1,0:T(8,128)S(1)} fusion(f32[36,64,4096]{2,1,0:T(8,128)} %bitcast.239, f32[64,4096]{1,0:T(8,128)S(1)} %fusion.58), kind=kLoop, calls=%fused_computation.8.clone.1 | loop fusion | flops 18726912 | bytes 39387136 | tf_op jit(solution)/shard_map/while/body/eval_jaxpr/reduce_sum | solution.py:160
  205.5 3.6 %convolution_bitcast_fusion.2 = f32[4,8,3,8,1024]{4,3,2,1,0:T(8,128)S(1)} fusion(f32[24,8,1,1]{0,1,3,2:T(8,128)S(1)} %get-tuple-element.721, f32[4,8,4,1024]{3,2,1,0:T(4,128)S(1)} %get-tuple-element.658, f32[4,8,4,1024]{3,2,1,0:T(4,128)S(1)} %get-tuple-element.659), kind=kOutput, calls=%fused_computation.9.clone.1 | convolution fusion | flops 75759616 | bytes 4195072 | tf_op jit(solution)/shard_map/while/body/eval_jaxpr/rn,clnb->clrb/dot_general | solution.py:89
  214.8 16.0 %fusion.57 = f32[4096,2304]{0,1:T(8,128)} fusion(bf16[2304,72]{1,0:T(8,128)(2,1)} %get-tuple-element.719, s32[4096]{0:T(1024)S(1)} %get-tuple-element.656), kind=kOutput, calls=%fused_computation.11.clone.1 | convolution fusion | flops 1359249408 | bytes 38096896 | tf_op jit(solution)/shard_map/while/body/eval_jaxpr/dot_general | solution.py:154
  230.9 14.8 %multiply_reduce_fusion.2 = f32[36,4096]{1,0:T(8,128)S(1)} fusion(f32[36,64,4096]{2,1,0:T(8,128)} %bitcast.239, f32[64,4096]{1,0:T(8,128)S(1)} %fusion.58), kind=kLoop, calls=%fused_computation.8.clone.1 | loop fusion | flops 18726912 | bytes 39387136 | tf_op jit(solution)/shard_map/while/body/eval_jaxpr/reduce_sum | solution.py:160
  246.3 3.6 %convolution_bitcast_fusion.2 = f32[4,8,3,8,1024]{4,3,2,1,0:T(8,128)S(1)} fusion(f32[24,8,1,1]{0,1,3,2:T(8,128)S(1)} %get-tuple-element.721, f32[4,8,4,1024]{3,2,1,0:T(4,128)S(1)} %get-tuple-element.658, f32[4,8,4,1024]{3,2,1,0:T(4,128)S(1)} %get-tuple-element.659), kind=kOutput, calls=%fused_computation.9.clone.1 | convolution fusion | flops 75759616 | bytes 4195072 | tf_op jit(solution)/shard_map/while/body/eval_jaxpr/rn,clnb->clrb/dot_general | solution.py:89
  254.1 8.7 %while.45 = (s32[]{:T(128)}, f32[64,72]{1,0:T(8,128)}, s32[4,4096]{1,0:T(4,128)S(1)}, f32[4096]{0:T(1024)S(1)}, s32[]{:T(128)}, /*index=5*/s32[]{:T(128)}, s32[]{:T(128)}, s32[]{:T(128)}) while((s32[]{:T(128)}, f32[64,72]{1,0:T(8,128)}, s32[4,4096]{1,0:T(4,128)S(1)}, f32[4096]{0:T(1024)S(1)}, s32[]{:T(128)}, /*index=5*/s32[]{:T(128)}, ...), condition=%wide.region_7.9_spmd.clone, body=%wide.region_6.8_spmd.clone.sunk | while | flops 227398656 | bytes 229525 | solution.py:202
  255.8 2.3 fusion.62
  258.1 2.3 fusion.62
  260.5 2.3 fusion.62
  263.7 48.1 %psum.7 = f32[4608]{0:T(1024)S(1)} all-reduce(f32[4608]{0:T(1024)S(1)} %reshape.352), channel_id=1, replica_groups=mesh['layer'=16,'plane'=32] {'layer'}, use_global_device_ids=true, to_apply=%region_8.10 | all-reduce | flops 4608 | bytes 36864 | tf_op jit(solution)/shard_map/psum | solution.py:206
  311.7 4.5 %collective-permute-start.5 = (f32[128]{0:T(128)S(1)}, f32[128]{0:T(128)S(1)}, u32[]{:S(2)}, u32[]{:S(2)}) collective-permute-start(f32[128]{0:T(128)S(1)} %get-tuple-element.525), channel_id=1, source_target_pairs={{0,2},{1,3},{2,4},{3,5},{4,6},{5,7},{6,8},{7,9},{8,10},{9,11},{10,... | collective-permute-start | bytes 1544 | tf_op jit(solution)/shard_map/ppermute | solution.py:15
  318.4 5.8 %collective-permute-start.7 = (f32[128]{0:T(128)S(1)}, f32[128]{0:T(128)S(1)}, u32[]{:S(2)}, u32[]{:S(2)}) collective-permute-start(f32[128]{0:T(128)S(1)} %get-tuple-element.523), channel_id=1, source_target_pairs={{1,0},{2,1},{3,2},{4,3},{5,4},{6,5},{7,6},{8,7},{9,8},{10,9},{11,1... | collective-permute-start | bytes 1544 | tf_op jit(solution)/shard_map/ppermute | solution.py:15
  (192 shorter events, 44.5 us)
Async XLA Ops:
  6.5 34.4 %copy-start.5 = (bf16[2,8,4096]{2,1,0:T(8,128)(2,1)S(1)}, bf16[2,8,4096]{2,1,0:T(8,128)(2,1)}, u32[]{:S(2)}) copy-start(bf16[2,8,4096]{2,1,0:T(8,128)(2,1)} %param.19) | copy-start | bytes 393220
  6.5 34.5 %copy-start.3 = (f32[8,4096]{1,0:T(8,128)S(1)}, f32[8,4096]{1,0:T(8,128)}, u32[]{:S(2)}) copy-start(f32[8,4096]{1,0:T(8,128)} %param.27) | copy-start | bytes 393220
  6.5 35.2 %copy-start.4 = (f32[8,4096]{1,0:T(8,128)S(1)}, f32[8,4096]{1,0:T(8,128)}, u32[]{:S(2)}) copy-start(f32[8,4096]{1,0:T(8,128)} %param.28) | copy-start | bytes 393220
  6.5 36.8 %copy-start.6 = (bf16[2,8,4096]{2,1,0:T(8,128)(2,1)S(1)}, bf16[2,8,4096]{2,1,0:T(8,128)(2,1)}, u32[]{:S(2)}) copy-start(bf16[2,8,4096]{2,1,0:T(8,128)(2,1)} %param.20) | copy-start | bytes 393220
  13.3 70.6 %copy-start.12 = (s32[4,128]{1,0:T(4,128)S(1)}, s32[4,128]{1,0:T(4,128)}, u32[]{:S(2)}) copy-start(s32[4,128]{1,0:T(4,128)} %param.22) | copy-start | bytes 6148
  16.5 68.0 %collective-permute-start = (bf16[4,8,128]{1,0,2:T(4,128)(2,1)S(1)}, bf16[4,8,128]{1,0,2:T(4,128)(2,1)S(1)}, u32[]{:S(2)}, u32[]{:S(2)}) collective-permute-start(bf16[4,8,128]{1,0,2:T(4,128)(2,1)S(1)} %select_bitcast_fusion.3), channel_id=1, source_target_pairs={{0,2},{1,3},{2,4},{3,5},{4,6},{5,7},{6,8},{7,9},{8,10},{9,11},{10,... | collective-permute-start | bytes 24584 | tf_op jit(solution)/shard_map/ppermute | solution.py:15
  24.2 60.4 %collective-permute-start.1 = (bf16[4,8,128]{1,0,2:T(4,128)(2,1)S(1)}, bf16[4,8,128]{1,0,2:T(4,128)(2,1)S(1)}, u32[]{:S(2)}, u32[]{:S(2)}) collective-permute-start(bf16[4,8,128]{1,0,2:T(4,128)(2,1)S(1)} %select_bitcast_fusion.2), channel_id=1, source_target_pairs={{0,1},{1,2},{2,3},{3,4},{4,5},{5,6},{6,7},{7,8},{8,9},{9,10},{10,1... | collective-permute-start | bytes 24584 | tf_op jit(solution)/shard_map/ppermute | solution.py:15
  30.8 53.9 %collective-permute-start.2 = (bf16[4,8,128]{1,0,2:T(4,128)(2,1)S(1)}, bf16[4,8,128]{1,0,2:T(4,128)(2,1)S(1)}, u32[]{:S(2)}, u32[]{:S(2)}) collective-permute-start(bf16[4,8,128]{1,0,2:T(4,128)(2,1)S(1)} %select_bitcast_fusion.1), channel_id=1, source_target_pairs={{1,0},{2,1},{3,2},{4,3},{5,4},{6,5},{7,6},{8,7},{9,8},{10,9},{11,1... | collective-permute-start | bytes 24584 | tf_op jit(solution)/shard_map/ppermute | solution.py:15
  38.5 51.3 %copy-start = (f32[8,4096]{1,0:T(8,128)S(1)}, f32[8,4096]{1,0:T(8,128)}, u32[]{:S(2)}) copy-start(f32[8,4096]{1,0:T(8,128)} %param.25) | copy-start | bytes 393220
  38.5 51.3 %copy-start.7 = (s32[4,4096]{1,0:T(4,128)S(1)}, s32[4,4096]{1,0:T(4,128)}, u32[]{:S(2)}) copy-start(s32[4,4096]{1,0:T(4,128)} %param.21) | copy-start | bytes 196612
  38.5 51.3 %copy-start.8 = (f32[24,8,1,1]{0,1,3,2:T(8,128)S(1)}, f32[24,8,1,1]{0,1,3,2:T(8,128)}, u32[]{:S(2)}) copy-start(f32[24,8,1,1]{0,1,3,2:T(8,128)} %constant.375) | copy-start | bytes 2308
  38.5 46.3 %collective-permute-start.3 = (bf16[4,8,128]{1,0,2:T(4,128)(2,1)S(1)}, bf16[4,8,128]{1,0,2:T(4,128)(2,1)S(1)}, u32[]{:S(2)}, u32[]{:S(2)}) collective-permute-start(bf16[4,8,128]{1,0,2:T(4,128)(2,1)S(1)} %select_bitcast_fusion), channel_id=1, source_target_pairs={{2,0},{3,1},{4,2},{5,3},{6,4},{7,5},{8,6},{9,7},{10,8},{11,9},{12,... | collective-permute-start | bytes 24584 | tf_op jit(solution)/shard_map/ppermute | solution.py:15
  83.9 4.3 %copy-start.1 = (f32[4096]{0:T(1024)}, f32[4096]{0:T(1024)S(1)}, u32[]{:S(2)}) copy-start(f32[4096]{0:T(1024)S(1)} %get-tuple-element.341) | copy-start | bytes 49156
  85.0 3.1 collective-permute-start.4
  89.8 163.3 %copy-start.2 = (f32[4096]{0:T(1024)S(1)}, f32[4096]{0:T(1024)}, u32[]{:S(2)}) copy-start(f32[4096]{0:T(1024)} %copy-done.1) | copy-start | bytes 49156
  89.8 163.3 %copy-start.9 = (f32[1,4096]{1,0:T(1,128)S(1)}, f32[1,4096]{1,0:T(1,128)}, u32[]{:S(2)}) copy-start(f32[1,4096]{1,0:T(1,128)} %get-tuple-element.501) | copy-start | bytes 49156
  89.8 163.3 %copy-start.10 = (f32[1,4096]{1,0:T(1,128)S(1)}, f32[1,4096]{1,0:T(1,128)}, u32[]{:S(2)}) copy-start(f32[1,4096]{1,0:T(1,128)} %get-tuple-element.502) | copy-start | bytes 49156
  89.8 163.3 %copy-start.11 = (f32[1,4096]{1,0:T(1,128)S(1)}, f32[1,4096]{1,0:T(1,128)}, u32[]{:S(2)}) copy-start(f32[1,4096]{1,0:T(1,128)} %get-tuple-element.503) | copy-start | bytes 49156
  252.9 73.5 %copy-start.16 = (s32[128]{0:T(128)S(1)}, s32[128]{0:T(128)}, u32[]{:S(2)}) copy-start(s32[128]{0:T(128)} %get-tuple-element.529) | copy-start | bytes 1540
  254.0 73.8 %copy-start.15 = (s32[128]{0:T(128)S(1)}, s32[128]{0:T(128)}, u32[]{:S(2)}) copy-start(s32[128]{0:T(128)} %get-tuple-element.528) | copy-start | bytes 1540
  254.0 75.1 %copy-start.14 = (s32[128]{0:T(128)S(1)}, s32[128]{0:T(128)}, u32[]{:S(2)}) copy-start(s32[128]{0:T(128)} %get-tuple-element.527) | copy-start | bytes 1540
  254.0 76.5 %copy-start.13 = (s32[128]{0:T(128)S(1)}, s32[128]{0:T(128)}, u32[]{:S(2)}) copy-start(s32[128]{0:T(128)} %get-tuple-element.526) | copy-start | bytes 1540
  311.7 14.7 %collective-permute-start.5 = (f32[128]{0:T(128)S(1)}, f32[128]{0:T(128)S(1)}, u32[]{:S(2)}, u32[]{:S(2)}) collective-permute-start(f32[128]{0:T(128)S(1)} %get-tuple-element.525), channel_id=1, source_target_pairs={{0,2},{1,3},{2,4},{3,5},{4,6},{5,7},{6,8},{7,9},{8,10},{9,11},{10,... | collective-permute-start | bytes 1544 | tf_op jit(solution)/shard_map/ppermute | solution.py:15
  316.2 11.5 %collective-permute-start.6 = (f32[128]{0:T(128)S(1)}, f32[128]{0:T(128)S(1)}, u32[]{:S(2)}, u32[]{:S(2)}) collective-permute-start(f32[128]{0:T(128)S(1)} %get-tuple-element.524), channel_id=1, source_target_pairs={{0,1},{1,2},{2,3},{3,4},{4,5},{5,6},{6,7},{7,8},{8,9},{9,10},{10,1... | collective-permute-start | bytes 1544 | tf_op jit(solution)/shard_map/ppermute | solution.py:15
  318.4 10.7 %collective-permute-start.7 = (f32[128]{0:T(128)S(1)}, f32[128]{0:T(128)S(1)}, u32[]{:S(2)}, u32[]{:S(2)}) collective-permute-start(f32[128]{0:T(128)S(1)} %get-tuple-element.523), channel_id=1, source_target_pairs={{1,0},{2,1},{3,2},{4,3},{5,4},{6,5},{7,6},{8,7},{9,8},{10,9},{11,1... | collective-permute-start | bytes 1544 | tf_op jit(solution)/shard_map/ppermute | solution.py:15
  324.2 6.3 %collective-permute-start.8 = (f32[128]{0:T(128)S(1)}, f32[128]{0:T(128)S(1)}, u32[]{:S(2)}, u32[]{:S(2)}) collective-permute-start(f32[128]{0:T(128)S(1)} %get-tuple-element.522), channel_id=1, source_target_pairs={{2,0},{3,1},{4,2},{5,3},{6,4},{7,5},{8,6},{9,7},{10,8},{11,9},{12,... | collective-permute-start | bytes 1544 | tf_op jit(solution)/shard_map/ppermute | solution.py:15
where the time goes:
time: 335 us; the launch traced here: 332 us
  blocking collectives  87.1 us (26%)
  matrix products  86.8 us (26%)
  other arithmetic  82.7 us (25%)
  local copies, waits for them, and re-layouts  33.9 us (10%)
  starting transfers between devices  31 us (9%)
  loops' own time  8.69 us (3%)
    dot_general x4, matrix products, one_block(): jnp.dot(level_table, high_select(corner_ids, high_count, jnp.bfloat16), p...  63.9 us
    reduce_sum x4, other arithmetic, one_block(): nodal_values = jnp.sum(picked * low_select(corner_ids)[None], axis=1)  59.2 us
    psum x1, blocking collectives, shards(): summed = lax.psum(partial_nodes, 'layer')  48.1 us
    all_gather x2, blocking collectives, entering_2(): everything = jax.tree.map(lambda part: lax.all_gather(part, axis), value)  39 us
    ppermute x9, starting transfers between devices, shifted(): lax.ppermute(value, axis, [(source, source + steps) for source in range(f...  31 us
    dot_general x4, matrix products, element_terms(): jnp.einsum('rn,clnb->clrb', basis, hexa_nodes, precision=lax.Precision.HI...  14.5 us
    gather x4, local copies, waits for them, and re-layouts, shards(): jnp.take(padded, shared[direction], axis=2)  11.8 us
    dot_general x4, matrix products, add_block(): jnp.dot(low_values, high_select(corner_ids, high_count, jnp.float32).T, p...  8.37 us
  transfers between devices with their start and end apart: 9, of which 2 were waited for; matrix products, arithmetic and copies ran while one was open for 5% of the time, Pallas kernels for 0%

commit v1 on v0

--- a/solution.py
+++ b/solution.py
@@ -203,7 +203,8 @@
         0, block_count, add_block, jnp.zeros((LOW_SPAN, high_count), jnp.float32)
     )
     partial_nodes = jnp.transpose(node_table).reshape(local_count)
-    summed = lax.psum(partial_nodes, "layer")
+    pieces = lax.all_gather(partial_nodes, "layer", axis=0, tiled=False)
+    summed = pieces.sum(axis=0)
     ghost_part = summed[owned_count:].reshape(4, slot_count)
     arriving = [
         shifted(ghost_part[3 - direction], "plane", -OFFSETS[direction]) for direction in range(4)

time: 335 us -> 304 us (0.907)
  blocking collectives: 87.1 us -> 56.5 us
    psum x1 -> x0, blocking collectives: 48.1 us -> none  [shards(): summed = lax.psum(partial_nodes, 'layer')]
    all_gather x0 -> x1, blocking collectives: none -> 17.5 us  [shards(): pieces = lax.all_gather(partial_nodes, 'layer', axis=0, tiled=False)]
  transfers between devices with their start and end apart: 9 -> 9, of which waited for: 2 -> 2; matrix products, arithmetic and copies ran while one was open for 5% -> 6% of each run, Pallas kernels for 0% -> 0%
where the time goes in v1:
time: 304 us; the launch traced here: 302 us
  matrix products  86.8 us (29%)
  other arithmetic  82.9 us (27%)
  blocking collectives  56.5 us (19%)
  local copies, waits for them, and re-layouts  33.9 us (11%)
  starting transfers between devices  31 us (10%)
  loops' own time  8.69 us (3%)
    dot_general x4, matrix products, one_block(): jnp.dot(level_table, high_select(corner_ids, high_count, jnp.bfloat16), p...  63.9 us
    reduce_sum x4, other arithmetic, one_block(): nodal_values = jnp.sum(picked * low_select(corner_ids)[None], axis=1)  59.2 us
    all_gather x2, blocking collectives, entering_2(): everything = jax.tree.map(lambda part: lax.all_gather(part, axis), value)  39 us
    ppermute x9, starting transfers between devices, shifted(): lax.ppermute(value, axis, [(source, source + steps) for source in range(f...  31 us
    all_gather x1, blocking collectives, shards(): pieces = lax.all_gather(partial_nodes, 'layer', axis=0, tiled=False)  17.5 us
    dot_general x4, matrix products, element_terms(): jnp.einsum('rn,clnb->clrb', basis, hexa_nodes, precision=lax.Precision.HI...  14.5 us
    gather x4, local copies, waits for them, and re-layouts, shards(): jnp.take(padded, shared[direction], axis=2)  11.8 us
    dot_general x4, matrix products, add_block(): jnp.dot(low_values, high_select(corner_ids, high_count, jnp.float32).T, p...  8.37 us
  transfers between devices with their start and end apart: 9, of which 2 were waited for; matrix products, arithmetic and copies ran while one was open for 6% of the time, Pallas kernels for 0%

profile of v1, /device:TPU:2, one launch (start us, length us, event | category | flops | bytes accessed | tf_op | source)
XLA Modules:
  0.0 302.1 jit_solution(6682381268800975701)
XLA Ops:
  1.9 4.6 %copy.48 = bf16[4,8,4096]{1,0,2:T(4,128)(2,1)} copy(bf16[4,8,4096]{2,1,0:T(8,128)(2,1)S(1)} %pad_maximum_fusion.1) | data formatting | bytes 524288 | tf_op jit(solution)/shard_map/concatenate | solution.py:135
  6.5 6.8 %concatenate.22 = bf16[4,8,4097]{1,0,2:T(4,128)(2,1)} pad(bf16[4,8,4096]{1,0,2:T(4,128)(2,1)} %copy.48, bf16[]{:T(256)} %constant.243.clone.1), padding=0_0x0_0x0_1 | pad | bytes 524354 | tf_op jit(solution)/shard_map/concatenate | solution.py:136
  13.3 3.0 gather_fusion
  16.5 4.5 %collective-permute-start = (bf16[4,8,128]{1,0,2:T(4,128)(2,1)S(1)}, bf16[4,8,128]{1,0,2:T(4,128)(2,1)S(1)}, u32[]{:S(2)}, u32[]{:S(2)}) collective-permute-start(bf16[4,8,128]{1,0,2:T(4,128)(2,1)S(1)} %select_bitcast_fusion.3), channel_id=1, source_target_pairs={{0,2},{1,3},{2,4},{3,5},{4,6},{5,7},{6,8},{7,9},{8,10},{9,11},{10,... | collective-permute-start | bytes 24584 | tf_op jit(solution)/shard_map/ppermute | solution.py:15
  21.0 2.9 gather_fusion.1
  24.2 3.5 %collective-permute-start.1 = (bf16[4,8,128]{1,0,2:T(4,128)(2,1)S(1)}, bf16[4,8,128]{1,0,2:T(4,128)(2,1)S(1)}, u32[]{:S(2)}, u32[]{:S(2)}) collective-permute-start(bf16[4,8,128]{1,0,2:T(4,128)(2,1)S(1)} %select_bitcast_fusion.2), channel_id=1, source_target_pairs={{0,1},{1,2},{2,3},{3,4},{4,5},{5,6},{6,7},{7,8},{8,9},{9,10},{10,1... | collective-permute-start | bytes 24584 | tf_op jit(solution)/shard_map/ppermute | solution.py:15
  27.7 2.9 gather_fusion.2
  30.8 4.5 %collective-permute-start.2 = (bf16[4,8,128]{1,0,2:T(4,128)(2,1)S(1)}, bf16[4,8,128]{1,0,2:T(4,128)(2,1)S(1)}, u32[]{:S(2)}, u32[]{:S(2)}) collective-permute-start(bf16[4,8,128]{1,0,2:T(4,128)(2,1)S(1)} %select_bitcast_fusion.1), channel_id=1, source_target_pairs={{1,0},{2,1},{3,2},{4,3},{5,4},{6,5},{7,6},{8,7},{9,8},{10,9},{11,1... | collective-permute-start | bytes 24584 | tf_op jit(solution)/shard_map/ppermute | solution.py:15
  35.3 2.9 gather_fusion.3
  38.5 2.4 collective-permute-start.3
  43.3 23.9 %all-gather = f32[16,1,4096]{2,1,0:T(1,128)S(1)} all-gather(f32[1,1,4096]{2,1,0:T(1,128)S(1)} %get-tuple-element.500), channel_id=1, replica_groups=mesh['layer'=16,'plane'=32] {'layer'}, dimensions={0}, use_global_device_ids=true | all-gather | bytes 278528 | tf_op jit(solution)/shard_map/all_gather | solution.py:20
  67.3 15.2 %all-gather.1 = f32[16,1,4096]{2,1,0:T(1,128)S(1)} all-gather(f32[1,1,4096]{2,1,0:T(1,128)S(1)} %get-tuple-element.496), channel_id=1, replica_groups=mesh['layer'=16,'plane'=32] {'layer'}, dimensions={0}, use_global_device_ids=true | all-gather | bytes 278528 | tf_op jit(solution)/shard_map/all_gather | solution.py:20
  89.8 163.1 %while.43 = (s32[]{:T(128)}, f32[4,8,1024]{2,1,0:T(8,128)S(1)}, s32[4]{0:T(128)S(1)}, f32[8,4096]{1,0:T(8,128)S(1)}, f32[2,4096]{1,0:T(2,128)}, /*index=5*/f32[2...) while((s32[]{:T(128)}, f32[4,8,1024]{2,1,0:T(8,128)S(1)}, ...), condition=%wide.region_5.7_spmd.clone, body=%wide.region_2.6_spmd.sunk.clone.sunk | while | flops 1458830336 | bytes 95925216 | solution.py:170
  92.4 16.0 %fusion.57 = f32[4096,2304]{0,1:T(8,128)} fusion(bf16[2304,72]{1,0:T(8,128)(2,1)} %get-tuple-element.719, s32[4096]{0:T(1024)S(1)} %get-tuple-element.656), kind=kOutput, calls=%fused_computation.11.clone.1 | convolution fusion | flops 1359249408 | bytes 38096896 | tf_op jit(solution)/shard_map/while/body/eval_jaxpr/dot_general | solution.py:154
  108.5 14.8 %multiply_reduce_fusion.2 = f32[36,4096]{1,0:T(8,128)S(1)} fusion(f32[36,64,4096]{2,1,0:T(8,128)} %bitcast.239, f32[64,4096]{1,0:T(8,128)S(1)} %fusion.58), kind=kLoop, calls=%fused_computation.8.clone.1 | loop fusion | flops 18726912 | bytes 39387136 | tf_op jit(solution)/shard_map/while/body/eval_jaxpr/reduce_sum | solution.py:160
  124.0 3.6 %convolution_bitcast_fusion.2 = f32[4,8,3,8,1024]{4,3,2,1,0:T(8,128)S(1)} fusion(f32[24,8,1,1]{0,1,3,2:T(8,128)S(1)} %get-tuple-element.721, f32[4,8,4,1024]{3,2,1,0:T(4,128)S(1)} %get-tuple-element.658, f32[4,8,4,1024]{3,2,1,0:T(4,128)S(1)} %get-tuple-element.659), kind=kOutput, calls=%fused_computation.9.clone.1 | convolution fusion | flops 75759616 | bytes 4195072 | tf_op jit(solution)/shard_map/while/body/eval_jaxpr/rn,clnb->clrb/dot_general | solution.py:89
  133.2 16.0 %fusion.57 = f32[4096,2304]{0,1:T(8,128)} fusion(bf16[2304,72]{1,0:T(8,128)(2,1)} %get-tuple-element.719, s32[4096]{0:T(1024)S(1)} %get-tuple-element.656), kind=kOutput, calls=%fused_computation.11.clone.1 | convolution fusion | flops 1359249408 | bytes 38096896 | tf_op jit(solution)/shard_map/while/body/eval_jaxpr/dot_general | solution.py:154
  149.3 14.8 %multiply_reduce_fusion.2 = f32[36,4096]{1,0:T(8,128)S(1)} fusion(f32[36,64,4096]{2,1,0:T(8,128)} %bitcast.239, f32[64,4096]{1,0:T(8,128)S(1)} %fusion.58), kind=kLoop, calls=%fused_computation.8.clone.1 | loop fusion | flops 18726912 | bytes 39387136 | tf_op jit(solution)/shard_map/while/body/eval_jaxpr/reduce_sum | solution.py:160
  164.7 3.6 %convolution_bitcast_fusion.2 = f32[4,8,3,8,1024]{4,3,2,1,0:T(8,128)S(1)} fusion(f32[24,8,1,1]{0,1,3,2:T(8,128)S(1)} %get-tuple-element.721, f32[4,8,4,1024]{3,2,1,0:T(4,128)S(1)} %get-tuple-element.658, f32[4,8,4,1024]{3,2,1,0:T(4,128)S(1)} %get-tuple-element.659), kind=kOutput, calls=%fused_computation.9.clone.1 | convolution fusion | flops 75759616 | bytes 4195072 | tf_op jit(solution)/shard_map/while/body/eval_jaxpr/rn,clnb->clrb/dot_general | solution.py:89
  174.0 16.0 %fusion.57 = f32[4096,2304]{0,1:T(8,128)} fusion(bf16[2304,72]{1,0:T(8,128)(2,1)} %get-tuple-element.719, s32[4096]{0:T(1024)S(1)} %get-tuple-element.656), kind=kOutput, calls=%fused_computation.11.clone.1 | convolution fusion | flops 1359249408 | bytes 38096896 | tf_op jit(solution)/shard_map/while/body/eval_jaxpr/dot_general | solution.py:154
  190.1 14.8 %multiply_reduce_fusion.2 = f32[36,4096]{1,0:T(8,128)S(1)} fusion(f32[36,64,4096]{2,1,0:T(8,128)} %bitcast.239, f32[64,4096]{1,0:T(8,128)S(1)} %fusion.58), kind=kLoop, calls=%fused_computation.8.clone.1 | loop fusion | flops 18726912 | bytes 39387136 | tf_op jit(solution)/shard_map/while/body/eval_jaxpr/reduce_sum | solution.py:160
  205.5 3.6 %convolution_bitcast_fusion.2 = f32[4,8,3,8,1024]{4,3,2,1,0:T(8,128)S(1)} fusion(f32[24,8,1,1]{0,1,3,2:T(8,128)S(1)} %get-tuple-element.721, f32[4,8,4,1024]{3,2,1,0:T(4,128)S(1)} %get-tuple-element.658, f32[4,8,4,1024]{3,2,1,0:T(4,128)S(1)} %get-tuple-element.659), kind=kOutput, calls=%fused_computation.9.clone.1 | convolution fusion | flops 75759616 | bytes 4195072 | tf_op jit(solution)/shard_map/while/body/eval_jaxpr/rn,clnb->clrb/dot_general | solution.py:89
  214.8 16.0 %fusion.57 = f32[4096,2304]{0,1:T(8,128)} fusion(bf16[2304,72]{1,0:T(8,128)(2,1)} %get-tuple-element.719, s32[4096]{0:T(1024)S(1)} %get-tuple-element.656), kind=kOutput, calls=%fused_computation.11.clone.1 | convolution fusion | flops 1359249408 | bytes 38096896 | tf_op jit(solution)/shard_map/while/body/eval_jaxpr/dot_general | solution.py:154
  230.9 14.8 %multiply_reduce_fusion.2 = f32[36,4096]{1,0:T(8,128)S(1)} fusion(f32[36,64,4096]{2,1,0:T(8,128)} %bitcast.239, f32[64,4096]{1,0:T(8,128)S(1)} %fusion.58), kind=kLoop, calls=%fused_computation.8.clone.1 | loop fusion | flops 18726912 | bytes 39387136 | tf_op jit(solution)/shard_map/while/body/eval_jaxpr/reduce_sum | solution.py:160
  246.3 3.6 %convolution_bitcast_fusion.2 = f32[4,8,3,8,1024]{4,3,2,1,0:T(8,128)S(1)} fusion(f32[24,8,1,1]{0,1,3,2:T(8,128)S(1)} %get-tuple-element.721, f32[4,8,4,1024]{3,2,1,0:T(4,128)S(1)} %get-tuple-element.658, f32[4,8,4,1024]{3,2,1,0:T(4,128)S(1)} %get-tuple-element.659), kind=kOutput, calls=%fused_computation.9.clone.1 | convolution fusion | flops 75759616 | bytes 4195072 | tf_op jit(solution)/shard_map/while/body/eval_jaxpr/rn,clnb->clrb/dot_general | solution.py:89
  254.1 8.7 %while.45 = (s32[]{:T(128)}, f32[64,72]{1,0:T(8,128)}, s32[4,4096]{1,0:T(4,128)S(1)}, f32[4096]{0:T(1024)S(1)}, s32[]{:T(128)}, /*index=5*/s32[]{:T(128)}, s32[]{:T(128)}, s32[]{:T(128)}) while((s32[]{:T(128)}, f32[64,72]{1,0:T(8,128)}, s32[4,4096]{1,0:T(4,128)S(1)}, f32[4096]{0:T(1024)S(1)}, s32[]{:T(128)}, /*index=5*/s32[]{:T(128)}, ...), condition=%wide.region_7.9_spmd.clone, body=%wide.region_6.8_spmd.clone.sunk | while | flops 227398656 | bytes 229525 | solution.py:202
  255.8 2.3 fusion.62
  258.1 2.3 fusion.62
  260.5 2.3 fusion.62
  263.7 17.5 %all-gather.2 = f32[16,1,4608]{2,1,0:T(1,128)S(1)} all-gather(f32[1,1,4608]{2,1,0:T(1,128)S(1)} %reshape.439), channel_id=1, replica_groups=mesh['layer'=16,'plane'=32] {'layer'}, dimensions={0}, use_global_device_ids=true | all-gather | bytes 313344 | tf_op jit(solution)/shard_map/all_gather | solution.py:206
  281.4 4.5 %collective-permute-start.5 = (f32[128]{0:T(128)S(1)}, f32[128]{0:T(128)S(1)}, u32[]{:S(2)}, u32[]{:S(2)}) collective-permute-start(f32[128]{0:T(128)S(1)} %get-tuple-element.525), channel_id=1, source_target_pairs={{0,2},{1,3},{2,4},{3,5},{4,6},{5,7},{6,8},{7,9},{8,10},{9,11},{10,... | collective-permute-start | bytes 1544 | tf_op jit(solution)/shard_map/ppermute | solution.py:15
  288.0 5.8 %collective-permute-start.7 = (f32[128]{0:T(128)S(1)}, f32[128]{0:T(128)S(1)}, u32[]{:S(2)}, u32[]{:S(2)}) collective-permute-start(f32[128]{0:T(128)S(1)} %get-tuple-element.523), channel_id=1, source_target_pairs={{1,0},{2,1},{3,2},{4,3},{5,4},{6,5},{7,6},{8,7},{9,8},{10,9},{11,1... | collective-permute-start | bytes 1544 | tf_op jit(solution)/shard_map/ppermute | solution.py:15
  (193 shorter events, 44.7 us)
Async XLA Ops:
  6.5 34.4 %copy-start.5 = (bf16[2,8,4096]{2,1,0:T(8,128)(2,1)S(1)}, bf16[2,8,4096]{2,1,0:T(8,128)(2,1)}, u32[]{:S(2)}) copy-start(bf16[2,8,4096]{2,1,0:T(8,128)(2,1)} %param.19) | copy-start | bytes 393220
  6.5 34.5 %copy-start.3 = (f32[8,4096]{1,0:T(8,128)S(1)}, f32[8,4096]{1,0:T(8,128)}, u32[]{:S(2)}) copy-start(f32[8,4096]{1,0:T(8,128)} %param.27) | copy-start | bytes 393220
  6.5 35.2 %copy-start.4 = (f32[8,4096]{1,0:T(8,128)S(1)}, f32[8,4096]{1,0:T(8,128)}, u32[]{:S(2)}) copy-start(f32[8,4096]{1,0:T(8,128)} %param.28) | copy-start | bytes 393220
  6.5 36.8 %copy-start.6 = (bf16[2,8,4096]{2,1,0:T(8,128)(2,1)S(1)}, bf16[2,8,4096]{2,1,0:T(8,128)(2,1)}, u32[]{:S(2)}) copy-start(bf16[2,8,4096]{2,1,0:T(8,128)(2,1)} %param.20) | copy-start | bytes 393220
  13.3 70.6 %copy-start.12 = (s32[4,128]{1,0:T(4,128)S(1)}, s32[4,128]{1,0:T(4,128)}, u32[]{:S(2)}) copy-start(s32[4,128]{1,0:T(4,128)} %param.22) | copy-start | bytes 6148
  16.5 68.0 %collective-permute-start = (bf16[4,8,128]{1,0,2:T(4,128)(2,1)S(1)}, bf16[4,8,128]{1,0,2:T(4,128)(2,1)S(1)}, u32[]{:S(2)}, u32[]{:S(2)}) collective-permute-start(bf16[4,8,128]{1,0,2:T(4,128)(2,1)S(1)} %select_bitcast_fusion.3), channel_id=1, source_target_pairs={{0,2},{1,3},{2,4},{3,5},{4,6},{5,7},{6,8},{7,9},{8,10},{9,11},{10,... | collective-permute-start | bytes 24584 | tf_op jit(solution)/shard_map/ppermute | solution.py:15
  24.2 60.4 %collective-permute-start.1 = (bf16[4,8,128]{1,0,2:T(4,128)(2,1)S(1)}, bf16[4,8,128]{1,0,2:T(4,128)(2,1)S(1)}, u32[]{:S(2)}, u32[]{:S(2)}) collective-permute-start(bf16[4,8,128]{1,0,2:T(4,128)(2,1)S(1)} %select_bitcast_fusion.2), channel_id=1, source_target_pairs={{0,1},{1,2},{2,3},{3,4},{4,5},{5,6},{6,7},{7,8},{8,9},{9,10},{10,1... | collective-permute-start | bytes 24584 | tf_op jit(solution)/shard_map/ppermute | solution.py:15
  30.8 53.9 %collective-permute-start.2 = (bf16[4,8,128]{1,0,2:T(4,128)(2,1)S(1)}, bf16[4,8,128]{1,0,2:T(4,128)(2,1)S(1)}, u32[]{:S(2)}, u32[]{:S(2)}) collective-permute-start(bf16[4,8,128]{1,0,2:T(4,128)(2,1)S(1)} %select_bitcast_fusion.1), channel_id=1, source_target_pairs={{1,0},{2,1},{3,2},{4,3},{5,4},{6,5},{7,6},{8,7},{9,8},{10,9},{11,1... | collective-permute-start | bytes 24584 | tf_op jit(solution)/shard_map/ppermute | solution.py:15
  38.5 51.3 %copy-start = (f32[8,4096]{1,0:T(8,128)S(1)}, f32[8,4096]{1,0:T(8,128)}, u32[]{:S(2)}) copy-start(f32[8,4096]{1,0:T(8,128)} %param.25) | copy-start | bytes 393220
  38.5 51.3 %copy-start.7 = (s32[4,4096]{1,0:T(4,128)S(1)}, s32[4,4096]{1,0:T(4,128)}, u32[]{:S(2)}) copy-start(s32[4,4096]{1,0:T(4,128)} %param.21) | copy-start | bytes 196612
  38.5 51.3 %copy-start.8 = (f32[24,8,1,1]{0,1,3,2:T(8,128)S(1)}, f32[24,8,1,1]{0,1,3,2:T(8,128)}, u32[]{:S(2)}) copy-start(f32[24,8,1,1]{0,1,3,2:T(8,128)} %constant.376) | copy-start | bytes 2308
  38.5 46.3 %collective-permute-start.3 = (bf16[4,8,128]{1,0,2:T(4,128)(2,1)S(1)}, bf16[4,8,128]{1,0,2:T(4,128)(2,1)S(1)}, u32[]{:S(2)}, u32[]{:S(2)}) collective-permute-start(bf16[4,8,128]{1,0,2:T(4,128)(2,1)S(1)} %select_bitcast_fusion), channel_id=1, source_target_pairs={{2,0},{3,1},{4,2},{5,3},{6,4},{7,5},{8,6},{9,7},{10,8},{11,9},{12,... | collective-permute-start | bytes 24584 | tf_op jit(solution)/shard_map/ppermute | solution.py:15
  83.9 4.3 %copy-start.1 = (f32[4096]{0:T(1024)}, f32[4096]{0:T(1024)S(1)}, u32[]{:S(2)}) copy-start(f32[4096]{0:T(1024)S(1)} %get-tuple-element.341) | copy-start | bytes 49156
  85.0 3.1 %collective-permute-start.4 = (bf16[4,4608]{1,0:T(4,128)(2,1)S(1)}, bf16[4,4608]{1,0:T(4,128)(2,1)S(1)}, u32[]{:S(2)}, u32[]{:S(2)}) collective-permute-start(bf16[4,4608]{1,0:T(4,128)(2,1)S(1)} %bitcast.276), channel_id=1, source_target_pairs={{32,0},{64,32},{96,64},{128,96},{160,128},{192,160},{224,192},{256... | collective-permute-start | bytes 110600 | tf_op jit(solution)/shard_map/ppermute | solution.py:15
  89.8 163.3 %copy-start.2 = (f32[4096]{0:T(1024)S(1)}, f32[4096]{0:T(1024)}, u32[]{:S(2)}) copy-start(f32[4096]{0:T(1024)} %copy-done.1) | copy-start | bytes 49156
  89.8 163.3 %copy-start.9 = (f32[1,4096]{1,0:T(1,128)S(1)}, f32[1,4096]{1,0:T(1,128)}, u32[]{:S(2)}) copy-start(f32[1,4096]{1,0:T(1,128)} %get-tuple-element.501) | copy-start | bytes 49156
  89.8 163.3 %copy-start.10 = (f32[1,4096]{1,0:T(1,128)S(1)}, f32[1,4096]{1,0:T(1,128)}, u32[]{:S(2)}) copy-start(f32[1,4096]{1,0:T(1,128)} %get-tuple-element.502) | copy-start | bytes 49156
  89.8 163.3 %copy-start.11 = (f32[1,4096]{1,0:T(1,128)S(1)}, f32[1,4096]{1,0:T(1,128)}, u32[]{:S(2)}) copy-start(f32[1,4096]{1,0:T(1,128)} %get-tuple-element.503) | copy-start | bytes 49156
  254.0 42.1 %copy-start.16 = (s32[128]{0:T(128)S(1)}, s32[128]{0:T(128)}, u32[]{:S(2)}) copy-start(s32[128]{0:T(128)} %get-tuple-element.529) | copy-start | bytes 1540
  254.0 43.4 %copy-start.15 = (s32[128]{0:T(128)S(1)}, s32[128]{0:T(128)}, u32[]{:S(2)}) copy-start(s32[128]{0:T(128)} %get-tuple-element.528) | copy-start | bytes 1540
  254.0 44.7 %copy-start.14 = (s32[128]{0:T(128)S(1)}, s32[128]{0:T(128)}, u32[]{:S(2)}) copy-start(s32[128]{0:T(128)} %get-tuple-element.527) | copy-start | bytes 1540
  254.0 46.1 %copy-start.13 = (s32[128]{0:T(128)S(1)}, s32[128]{0:T(128)}, u32[]{:S(2)}) copy-start(s32[128]{0:T(128)} %get-tuple-element.526) | copy-start | bytes 1540
  281.4 14.7 %collective-permute-start.5 = (f32[128]{0:T(128)S(1)}, f32[128]{0:T(128)S(1)}, u32[]{:S(2)}, u32[]{:S(2)}) collective-permute-start(f32[128]{0:T(128)S(1)} %get-tuple-element.525), channel_id=1, source_target_pairs={{0,2},{1,3},{2,4},{3,5},{4,6},{5,7},{6,8},{7,9},{8,10},{9,11},{10,... | collective-permute-start | bytes 1544 | tf_op jit(solution)/shard_map/ppermute | solution.py:15
  285.9 11.5 %collective-permute-start.6 = (f32[128]{0:T(128)S(1)}, f32[128]{0:T(128)S(1)}, u32[]{:S(2)}, u32[]{:S(2)}) collective-permute-start(f32[128]{0:T(128)S(1)} %get-tuple-element.524), channel_id=1, source_target_pairs={{0,1},{1,2},{2,3},{3,4},{4,5},{5,6},{6,7},{7,8},{8,9},{9,10},{10,1... | collective-permute-start | bytes 1544 | tf_op jit(solution)/shard_map/ppermute | solution.py:15
  288.0 10.7 %collective-permute-start.7 = (f32[128]{0:T(128)S(1)}, f32[128]{0:T(128)S(1)}, u32[]{:S(2)}, u32[]{:S(2)}) collective-permute-start(f32[128]{0:T(128)S(1)} %get-tuple-element.523), channel_id=1, source_target_pairs={{1,0},{2,1},{3,2},{4,3},{5,4},{6,5},{7,6},{8,7},{9,8},{10,9},{11,1... | collective-permute-start | bytes 1544 | tf_op jit(solution)/shard_map/ppermute | solution.py:15
  293.9 6.3 %collective-permute-start.8 = (f32[128]{0:T(128)S(1)}, f32[128]{0:T(128)S(1)}, u32[]{:S(2)}, u32[]{:S(2)}) collective-permute-start(f32[128]{0:T(128)S(1)} %get-tuple-element.522), channel_id=1, source_target_pairs={{2,0},{3,1},{4,2},{5,3},{6,4},{7,5},{8,6},{9,7},{10,8},{11,9},{12,... | collective-permute-start | bytes 1544 | tf_op jit(solution)/shard_map/ppermute | solution.py:15
